TPU v7x, 32 devices: a whole 2x2x4 slice. The times are simulated.
32 devices in a mesh: groups: 2 (over x), tensor: 4 (over y, core), section: 4 (over z).
Axes of the slice: x: 2, y: 2, z: 4, core: 2. Of those that a mesh axis runs over, the one named last changes fastest.
Arguments:
- prompt: bfloat16 [128, 8192], P(('groups', 'section'), 'tensor'), parts along dimension 0, may hold values from -6 to 6
- norm_gain: float32 [8, 8192], P(('groups', 'section')), parts along dimension 0, may hold values from 0.5 to 1.5
- kept_ranks: int32 [8, 3], P(('groups', 'section')), parts along dimension 0, may hold values from 128 to 512, as said below
- gate_left: bfloat16 [8, 512, 8192], P('groups', 'tensor', 'section'), parts along dimension 0, may hold values from -0.0625 to 0.0625
- up_left: bfloat16 [8, 512, 8192], P('groups', 'tensor', 'section'), parts along dimension 0, may hold values from -0.0625 to 0.0625
- gate_right: bfloat16 [8, 512, 14336], P('groups', 'tensor', 'section'), parts along dimension 0, may hold values from -0.375 to 0.375
- up_right: bfloat16 [8, 512, 14336], P('groups', 'tensor', 'section'), parts along dimension 0, may hold values from -0.375 to 0.375
- down_left: bfloat16 [8, 512, 14336], P('groups', 'tensor', 'section'), parts along dimension 0, may hold values from -0.046875 to 0.046875
- down_right: bfloat16 [8, 8192, 512], P('groups', 'tensor', 'section'), parts along dimension 0, may hold values from -0.5 to 0.5
Outputs:
- final_stream: bfloat16 [128, 8192], P(('groups', 'section'), 'tensor'), parts along dimension 0
There are 2 independent parts, one for each index of `groups`. A program takes and returns all parts, laid end to end along the dimension named above; each array names one. Nothing has to cross between parts.
Inputs may be any that keep to these rules, and one draw needn't show every extreme that they name: `kept_ranks`: column 0, 1, 2 holds the rank kept for the gate, up and down matrices; the value 512 occurs in every draw.
All inputs are finite; a program needn't handle non-finite values.
Results may differ from a plain program's by a relative error of at most 0.035.
Values may be sent and summed in bfloat16 or wider, within the bound.
No kernel may reach another device: no remote copies, remote signals or barrier semaphores. Data moves between devices by JAX's collectives and lax.ppermute only.
A program may use at most 128 MiB of HBM per device.

v0:
```python
import jax
import jax.numpy as jnp
from jax import lax
from jax.sharding import PartitionSpec as P

RMAX = 512


def from_behind(block, axis, distance):
    devices = range(lax.axis_size(axis))
    route = [(i - distance, i) for i in devices if i - distance in devices]
    return lax.ppermute(block, axis, route)


def broadcast(array, axis, root):
    mine = lax.axis_index(axis) == root
    return lax.psum(jnp.where(mine, array, jnp.zeros_like(array)), axis)


def contract_last(left_side, right_side):
    return lax.dot_general(
        left_side, right_side, (((1,), (1,)), ((), ())), preferred_element_type=jnp.float32
    )


def body(
    prompt, norm_gain, kept_ranks, gate_left, up_left, gate_right, up_right, down_left, down_right
):
    section_count = lax.axis_size("section")
    tensor_rank = lax.axis_index("tensor")
    section_rank = lax.axis_index("section")
    gate_rows, up_rows, down_cols = (
        lax.all_to_all(gate_left, "section", split_axis=0, concat_axis=2, tiled=True),
        lax.all_to_all(up_left, "section", split_axis=0, concat_axis=2, tiled=True),
        lax.all_to_all(down_right, "section", split_axis=0, concat_axis=2, tiled=True),
    )
    gate_cols, up_cols, down_rows = (
        lax.all_to_all(
            lax.all_to_all(gate_right, "tensor", split_axis=2, concat_axis=1, tiled=True),
            "section",
            split_axis=0,
            concat_axis=2,
            tiled=True,
        ),
        lax.all_to_all(
            lax.all_to_all(up_right, "tensor", split_axis=2, concat_axis=1, tiled=True),
            "section",
            split_axis=0,
            concat_axis=2,
            tiled=True,
        ),
        lax.all_to_all(
            lax.all_to_all(down_left, "tensor", split_axis=2, concat_axis=1, tiled=True),
            "section",
            split_axis=0,
            concat_axis=2,
            tiled=True,
        ),
    )
    gate_rows, up_rows, down_cols = (gate_rows[0], up_rows[0], down_cols[0])
    gate_cols, up_cols, down_rows = (gate_cols[0], up_cols[0], down_rows[0])
    rank_block = gate_rows.shape[0]
    column_block = down_cols.shape[0]
    micro_rows = prompt.shape[0]
    positions = tensor_rank * rank_block + jnp.arange(rank_block, dtype=jnp.int32)
    gate_mask = (positions < kept_ranks[0, 0]).astype(jnp.float32)
    up_mask = (positions < kept_ranks[0, 1]).astype(jnp.float32)
    down_mask = (jnp.arange(RMAX, dtype=jnp.int32) < kept_ranks[0, 2]).astype(jnp.float32)
    norm_scale = norm_gain[0]
    own_start = tensor_rank * column_block
    prompt_rows = lax.all_gather(prompt, "section", axis=0, tiled=True)

    def layer_step(stream):
        float_stream = stream.astype(jnp.float32)
        variance = jnp.mean(float_stream * float_stream, axis=-1, keepdims=True)
        normed = (float_stream * lax.rsqrt(variance + 1e-05) * norm_scale).astype(jnp.bfloat16)
        gate_part = (contract_last(normed, gate_rows) * gate_mask).astype(jnp.bfloat16)
        up_part = (contract_last(normed, up_rows) * up_mask).astype(jnp.bfloat16)
        gate_low, up_low = (
            lax.all_gather(gate_part, "tensor", axis=1, tiled=True),
            lax.all_gather(up_part, "tensor", axis=1, tiled=True),
        )
        gate_values = jnp.dot(gate_low, gate_cols, preferred_element_type=jnp.float32)
        up_values = jnp.dot(up_low, up_cols, preferred_element_type=jnp.float32)
        hidden = (jax.nn.silu(gate_values) * up_values).astype(jnp.bfloat16)
        summed = lax.psum(contract_last(hidden, down_rows), "tensor")
        down_low = (summed * down_mask).astype(jnp.bfloat16)
        branch = contract_last(down_low, down_cols)
        own_columns = lax.dynamic_slice_in_dim(float_stream, own_start, column_block, 1)
        return (own_columns + branch).astype(jnp.bfloat16)

    incoming = jnp.zeros((micro_rows, column_block), jnp.bfloat16)
    results = jnp.zeros((micro_rows * section_count, column_block), jnp.bfloat16)

    def tick_body(tick_index, carry):
        incoming, results = carry
        entering = lax.dynamic_slice_in_dim(
            prompt_rows, jnp.minimum(tick_index, section_count - 1) * micro_rows, micro_rows, 0
        )
        current = jnp.where((section_rank == 0) & (tick_index < section_count), entering, incoming)
        stream = lax.all_gather(current, "tensor", axis=1, tiled=True)
        new_part = layer_step(stream)
        incoming = from_behind(new_part, "section", 1)
        finished = tick_index - (section_count - 1)
        slot_start = jnp.maximum(finished, 0) * micro_rows
        updated = lax.dynamic_update_slice_in_dim(results, new_part, slot_start, 0)
        results = jnp.where((section_rank == section_count - 1) & (finished >= 0), updated, results)
        return (incoming, results)

    incoming, results = lax.fori_loop(0, 2 * section_count - 1, tick_body, (incoming, results))
    delivered = broadcast(results, "section", section_count - 1)
    return lax.dynamic_slice_in_dim(delivered, section_rank * micro_rows, micro_rows, 0)


def solution(mesh):
    in_specs = (
        P(("groups", "section"), "tensor"),
        P(("groups", "section"), None),
        P(("groups", "section"), None),
        P("groups", "tensor", "section"),
        P("groups", "tensor", "section"),
        P("groups", "tensor", "section"),
        P("groups", "tensor", "section"),
        P("groups", "tensor", "section"),
        P("groups", "tensor", "section"),
    )
    out_specs = P(("groups", "section"), "tensor")
    return jax.shard_map(body, mesh=mesh, in_specs=in_specs, out_specs=out_specs, check_vma=False)
```

profile of v0, /device:TPU:4, one launch (start us, length us, event | category | flops | bytes accessed | tf_op | source)
XLA Modules:
  0.0 1001.7 jit_solution(816205238414276463)
XLA Ops:
  6.5 6.8 copy.26
  18.1 6.9 copy.30
  25.0 33.2 %all-to-all-done.1 = bf16[4,128,3584]{1,0,2:T(4,128)(2,1)} async-done(((bf16[4,128,3584]{1,0,2:T(4,128)(2,1)}), bf16[4,128,3584]{1,0,2:T(4,128)(2,1)}, u32[]{:S(2)}, u32[]{:S(2)}) %all-to-all-start.1) | async-done | bytes 3670048 | tf_op jit(solution)/shard_map/all_to_all | solution.py:39
  58.2 7.0 all-to-all-start.4
  65.1 6.9 copy.33
  72.0 34.1 %all-to-all-done.4 = bf16[4,128,3584]{1,0,2:T(4,128)(2,1)} async-done(((bf16[4,128,3584]{1,0,2:T(4,128)(2,1)}), bf16[4,128,3584]{1,0,2:T(4,128)(2,1)}, u32[]{:S(2)}, u32[]{:S(2)}) %all-to-all-start.4) | async-done | bytes 3670048 | tf_op jit(solution)/shard_map/all_to_all | solution.py:46
  106.1 48.1 %all_to_all.144 = bf16[4,128,3584]{1,0,2:T(4,128)(2,1)} all-to-all(bf16[4,128,3584]{1,0,2:T(4,128)(2,1)} %copy.33), channel_id=1, replica_groups=mesh['groups'=2,'tensor'=4,'section'=4] {'tensor'}, dimensions={2} | all-to-all | bytes 7340032 | tf_op jit(solution)/shard_map/all_to_all | solution.py:53
  154.2 54.0 %all_to_all.145 = bf16[4,128,2048]{2,1,0:T(8,128)(2,1)} all-to-all(bf16[4,128,2048]{2,1,0:T(8,128)(2,1)S(1)} %copy-done.6), channel_id=1, replica_groups=mesh['groups'=2,'tensor'=4,'section'=4] {'section'}, dimensions={0} | all-to-all | bytes 4194304 | tf_op jit(solution)/shard_map/all_to_all | solution.py:33
  208.2 51.0 %all_to_all.146 = bf16[4,128,2048]{2,1,0:T(8,128)(2,1)} all-to-all(bf16[4,128,2048]{2,1,0:T(8,128)(2,1)S(1)} %copy-done.7), channel_id=1, replica_groups=mesh['groups'=2,'tensor'=4,'section'=4] {'section'}, dimensions={0} | all-to-all | bytes 4194304 | tf_op jit(solution)/shard_map/all_to_all | solution.py:34
  262.8 6.9 copy.27
  269.7 40.3 %all-to-all-done.8 = bf16[4,2048,128]{2,1,0:T(8,128)(2,1)S(1)} async-done(((bf16[4,2048,128]{2,1,0:T(8,128)(2,1)}), bf16[4,2048,128]{2,1,0:T(8,128)(2,1)S(1)}, u32[]{:S(2)}, u32[]{:S(2)}) %all-to-all-start.8) | async-done | bytes 2097184 | tf_op jit(solution)/shard_map/all_to_all | solution.py:35
  316.1 6.9 copy.31
  323.0 74.6 %all-to-all-done.2 = bf16[4,512,896]{2,1,0:T(8,128)(2,1)} async-done(((bf16[4,512,896]{2,1,0:T(8,128)(2,1)}), bf16[4,512,896]{2,1,0:T(8,128)(2,1)}, u32[]{:S(2)}, u32[]{:S(2)}) %all-to-all-start.2) | async-done | bytes 3670048 | tf_op jit(solution)/shard_map/all_to_all | solution.py:38
  402.4 7.0 copy.34
  409.3 74.6 %all-to-all-done.5 = bf16[4,512,896]{2,1,0:T(8,128)(2,1)} async-done(((bf16[4,512,896]{2,1,0:T(8,128)(2,1)}), bf16[4,512,896]{2,1,0:T(8,128)(2,1)}, u32[]{:S(2)}, u32[]{:S(2)}) %all-to-all-start.5) | async-done | bytes 3670048 | tf_op jit(solution)/shard_map/all_to_all | solution.py:45
  488.8 89.0 %all_gather.33 = bf16[64,2048]{1,0:T(8,128)(2,1)S(1)} all-gather(bf16[16,2048]{1,0:T(8,128)(2,1)S(1)} %copy-done.8), channel_id=1, replica_groups=mesh['groups'=2,'tensor'=4,'section'=4] {'section'}, dimensions={0}, use_global_device_ids=true | all-gather | bytes 327680 | tf_op jit(solution)/shard_map/all_gather | solution.py:71
  585.9 9.7 copy.36
  597.4 6.0 copy.28
  603.3 5.9 copy.37
  609.2 6.0 copy.32
  615.2 6.0 copy.38
  621.2 6.0 copy.35
  627.2 6.0 copy.39
  633.2 321.8 %while.19 = (s32[]{:T(128)}, bf16[16,2048]{1,0:T(8,128)(2,1)S(1)}, bf16[64,2048]{1,0:T(8,128)(2,1)S(1)}, pred[]{:T(512)}, bf16[64,2048]{1,0:T(8,128)(2,1)S(1)}, ...) while((s32[]{:T(128)}, bf16[16,2048]{1,0:T(8,128)(2,1)S(1)}, ...), condition=%wide.region_3.4_spmd.clone.clone, body=%wide.region_0.3_spmd.clone.clone.sunk | while | flops 278906656 | bytes 35412760 | solution.py:110
  633.3 5.8 all_gather.43
  640.8 5.2 all_gather.45
  648.9 5.2 all_gather.44
  659.3 10.9 %psum.25 = f32[16,512]{1,0:T(8,128)S(1)} all-reduce(f32[16,512]{1,0:T(8,128)S(1)} %fusion.54), channel_id=1, replica_groups=mesh['groups'=2,'tensor'=4,'section'=4] {'tensor'}, use_global_device_ids=true, to_apply=%region_2.2 | all-reduce | flops 8192 | bytes 65536 | tf_op jit(solution)/shard_map/while/body/eval_jaxpr/psum | solution.py:86
  677.8 5.8 all_gather.43
  685.3 5.2 all_gather.45
  693.4 5.2 all_gather.44
  703.9 11.4 %psum.25 = f32[16,512]{1,0:T(8,128)S(1)} all-reduce(f32[16,512]{1,0:T(8,128)S(1)} %fusion.54), channel_id=1, replica_groups=mesh['groups'=2,'tensor'=4,'section'=4] {'tensor'}, use_global_device_ids=true, to_apply=%region_2.2 | all-reduce | flops 8192 | bytes 65536 | tf_op jit(solution)/shard_map/while/body/eval_jaxpr/psum | solution.py:86
  724.3 5.8 all_gather.43
  731.8 5.2 all_gather.45
  750.3 10.9 %psum.25 = f32[16,512]{1,0:T(8,128)S(1)} all-reduce(f32[16,512]{1,0:T(8,128)S(1)} %fusion.54), channel_id=1, replica_groups=mesh['groups'=2,'tensor'=4,'section'=4] {'tensor'}, use_global_device_ids=true, to_apply=%region_2.2 | all-reduce | flops 8192 | bytes 65536 | tf_op jit(solution)/shard_map/while/body/eval_jaxpr/psum | solution.py:86
  770.2 5.8 all_gather.43
  785.8 5.2 all_gather.44
  796.3 11.4 %psum.25 = f32[16,512]{1,0:T(8,128)S(1)} all-reduce(f32[16,512]{1,0:T(8,128)S(1)} %fusion.54), channel_id=1, replica_groups=mesh['groups'=2,'tensor'=4,'section'=4] {'tensor'}, use_global_device_ids=true, to_apply=%region_2.2 | all-reduce | flops 8192 | bytes 65536 | tf_op jit(solution)/shard_map/while/body/eval_jaxpr/psum | solution.py:86
  816.7 5.8 all_gather.43
  824.2 5.2 all_gather.45
  842.7 10.9 %psum.25 = f32[16,512]{1,0:T(8,128)S(1)} all-reduce(f32[16,512]{1,0:T(8,128)S(1)} %fusion.54), channel_id=1, replica_groups=mesh['groups'=2,'tensor'=4,'section'=4] {'tensor'}, use_global_device_ids=true, to_apply=%region_2.2 | all-reduce | flops 8192 | bytes 65536 | tf_op jit(solution)/shard_map/while/body/eval_jaxpr/psum | solution.py:86
  862.6 5.8 all_gather.43
  878.2 5.2 all_gather.44
  888.7 11.4 %psum.25 = f32[16,512]{1,0:T(8,128)S(1)} all-reduce(f32[16,512]{1,0:T(8,128)S(1)} %fusion.54), channel_id=1, replica_groups=mesh['groups'=2,'tensor'=4,'section'=4] {'tensor'}, use_global_device_ids=true, to_apply=%region_2.2 | all-reduce | flops 8192 | bytes 65536 | tf_op jit(solution)/shard_map/while/body/eval_jaxpr/psum | solution.py:86
  909.1 5.8 all_gather.43
  916.6 5.2 all_gather.45
  935.1 10.9 %psum.25 = f32[16,512]{1,0:T(8,128)S(1)} all-reduce(f32[16,512]{1,0:T(8,128)S(1)} %fusion.54), channel_id=1, replica_groups=mesh['groups'=2,'tensor'=4,'section'=4] {'tensor'}, use_global_device_ids=true, to_apply=%region_2.2 | all-reduce | flops 8192 | bytes 65536 | tf_op jit(solution)/shard_map/while/body/eval_jaxpr/psum | solution.py:86
  955.8 37.6 %all-reduce.2.cloned.1.call-done = bf16[64,2048]{1,0:T(8,128)(2,1)} async-done(((bf16[64,2048]{1,0:T(8,128)(2,1)}), bf16[64,2048]{1,0:T(8,128)(2,1)}) %all-reduce.2.cloned.1.call-update) | async-done | bytes 262160 | tf_op jit(solution)/shard_map/psum | solution.py:17
  (153 shorter events, 192.6 us)
Async XLA Ops:
  13.4 44.8 %all-to-all-start.1 = ((bf16[4,128,3584]{1,0,2:T(4,128)(2,1)}), bf16[4,128,3584]{1,0,2:T(4,128)(2,1)}, u32[]{:S(2)}, u32[]{:S(2)}) async-start(bf16[4,128,3584]{1,0,2:T(4,128)(2,1)} %copy.26), calls=%async_computation.1 | async-start | bytes 7340032 | tf_op jit(solution)/shard_map/all_to_all | solution.py:39
  58.2 48.0 %all-to-all-start.4 = ((bf16[4,128,3584]{1,0,2:T(4,128)(2,1)}), bf16[4,128,3584]{1,0,2:T(4,128)(2,1)}, u32[]{:S(2)}, u32[]{:S(2)}) async-start(bf16[4,128,3584]{1,0,2:T(4,128)(2,1)} %copy.30), calls=%async_computation.4 | async-start | bytes 7340032 | tf_op jit(solution)/shard_map/all_to_all | solution.py:46
  72.0 82.2 %copy-start.6 = (bf16[4,128,2048]{2,1,0:T(8,128)(2,1)S(1)}, bf16[4,128,2048]{2,1,0:T(8,128)(2,1)}, u32[]{:S(2)}) copy-start(bf16[4,128,2048]{2,1,0:T(8,128)(2,1)} %param.14) | copy-start | bytes 6291460
  154.2 54.0 %copy-start.7 = (bf16[4,128,2048]{2,1,0:T(8,128)(2,1)S(1)}, bf16[4,128,2048]{2,1,0:T(8,128)(2,1)}, u32[]{:S(2)}) copy-start(bf16[4,128,2048]{2,1,0:T(8,128)(2,1)} %param.15) | copy-start | bytes 6291460
  259.2 50.8 %all-to-all-start.8 = ((bf16[4,2048,128]{2,1,0:T(8,128)(2,1)}), bf16[4,2048,128]{2,1,0:T(8,128)(2,1)S(1)}, u32[]{:S(2)}, u32[]{:S(2)}) async-start(bf16[4,2048,128]{2,1,0:T(8,128)(2,1)} %param.19), calls=%async_computation.8 | async-start | bytes 4194304 | tf_op jit(solution)/shard_map/all_to_all | solution.py:35
  310.0 1.3 copy-start.1
  311.3 86.3 %all-to-all-start.2 = ((bf16[4,512,896]{2,1,0:T(8,128)(2,1)}), bf16[4,512,896]{2,1,0:T(8,128)(2,1)}, u32[]{:S(2)}, u32[]{:S(2)}) async-start(bf16[4,512,896]{2,1,0:T(8,128)(2,1)} %bitcast.83), calls=%async_computation.2 | async-start | bytes 7340032 | tf_op jit(solution)/shard_map/all_to_all | solution.py:38
  397.6 86.3 %all-to-all-start.5 = ((bf16[4,512,896]{2,1,0:T(8,128)(2,1)}), bf16[4,512,896]{2,1,0:T(8,128)(2,1)}, u32[]{:S(2)}, u32[]{:S(2)}) async-start(bf16[4,512,896]{2,1,0:T(8,128)(2,1)} %bitcast.82), calls=%async_computation.5 | async-start | bytes 7340032 | tf_op jit(solution)/shard_map/all_to_all | solution.py:45
  483.9 5.0 copy-start.8
  483.9 94.0 %copy-start.9 = (s32[1,3]{1,0:T(1,128)S(1)}, s32[1,3]{1,0:T(1,128)}, u32[]{:S(2)}) copy-start(s32[1,3]{1,0:T(1,128)} %param.13) | copy-start | bytes 40
  483.9 94.6 %copy-start.4 = (bf16[4,128,2048]{2,1,0:T(8,128)(2,1)S(1)}, bf16[4,128,2048]{2,1,0:T(8,128)(2,1)}, u32[]{:S(2)}) copy-start(bf16[4,128,2048]{2,1,0:T(8,128)(2,1)} %all_to_all.145) | copy-start | bytes 6291460
  483.9 137.3 %all-to-all-start.7 = ((bf16[4,512,896]{2,1,0:T(8,128)(2,1)}), bf16[4,512,896]{2,1,0:T(8,128)(2,1)}, u32[]{:S(2)}, u32[]{:S(2)}) async-start(bf16[4,512,896]{2,1,0:T(8,128)(2,1)} %bitcast.80), calls=%async_computation.7 | async-start | bytes 7340032 | tf_op jit(solution)/shard_map/all_to_all | solution.py:52
  488.8 504.6 %all-reduce.2.cloned.1.call-start = ((), (), s32[]{:S(2)}) async-start(), calls=%async_computation.9 | async-start | bytes 524288 | tf_op jit(solution)/shard_map/psum | solution.py:17
  578.5 3.1 copy-start.3
  581.5 4.4 copy-start.2
  627.2 6.0 copy-start.5
  639.3 14.8 %copy-start = (bf16[512,3584]{1,0:T(8,128)(2,1)S(1)}, bf16[512,3584]{1,0:T(8,128)(2,1)}, u32[]{:S(2)}) copy-start(bf16[512,3584]{1,0:T(8,128)(2,1)} %get-tuple-element.710) | copy-start | bytes 11010052 | tf_op jit(solution)/shard_map/while
  673.0 4.8 collective-permute-start
  683.9 14.8 %copy-start = (bf16[512,3584]{1,0:T(8,128)(2,1)S(1)}, bf16[512,3584]{1,0:T(8,128)(2,1)}, u32[]{:S(2)}) copy-start(bf16[512,3584]{1,0:T(8,128)(2,1)} %get-tuple-element.710) | copy-start | bytes 11010052 | tf_op jit(solution)/shard_map/while
  718.1 6.2 collective-permute-start
  730.3 14.8 %copy-start = (bf16[512,3584]{1,0:T(8,128)(2,1)S(1)}, bf16[512,3584]{1,0:T(8,128)(2,1)}, u32[]{:S(2)}) copy-start(bf16[512,3584]{1,0:T(8,128)(2,1)} %get-tuple-element.710) | copy-start | bytes 11010052 | tf_op jit(solution)/shard_map/while
  764.0 6.2 collective-permute-start
  776.2 14.8 %copy-start = (bf16[512,3584]{1,0:T(8,128)(2,1)S(1)}, bf16[512,3584]{1,0:T(8,128)(2,1)}, u32[]{:S(2)}) copy-start(bf16[512,3584]{1,0:T(8,128)(2,1)} %get-tuple-element.710) | copy-start | bytes 11010052 | tf_op jit(solution)/shard_map/while
  810.5 6.2 collective-permute-start
  822.7 14.8 %copy-start = (bf16[512,3584]{1,0:T(8,128)(2,1)S(1)}, bf16[512,3584]{1,0:T(8,128)(2,1)}, u32[]{:S(2)}) copy-start(bf16[512,3584]{1,0:T(8,128)(2,1)} %get-tuple-element.710) | copy-start | bytes 11010052 | tf_op jit(solution)/shard_map/while
  856.4 6.2 collective-permute-start
  868.6 14.8 %copy-start = (bf16[512,3584]{1,0:T(8,128)(2,1)S(1)}, bf16[512,3584]{1,0:T(8,128)(2,1)}, u32[]{:S(2)}) copy-start(bf16[512,3584]{1,0:T(8,128)(2,1)} %get-tuple-element.710) | copy-start | bytes 11010052 | tf_op jit(solution)/shard_map/while
  902.9 6.2 collective-permute-start
  915.1 14.8 %copy-start = (bf16[512,3584]{1,0:T(8,128)(2,1)S(1)}, bf16[512,3584]{1,0:T(8,128)(2,1)}, u32[]{:S(2)}) copy-start(bf16[512,3584]{1,0:T(8,128)(2,1)} %get-tuple-element.710) | copy-start | bytes 11010052 | tf_op jit(solution)/shard_map/while
  948.8 6.2 collective-permute-start
Sparse Core Ops, SparseCore 0:
  955.9 37.4 all-reduce.1
where the time goes:
time: 1010 us; the launch traced here: 1000 us
  blocking collectives  433 us (43%)
  waiting for transfers between devices  308 us (30%)
  local copies, waits for them, and re-layouts  99.4 us (10%)
  matrix products  73.3 us (7%)
  starting transfers between devices  58.3 us (6%)
  other arithmetic  16.3 us (2%)
  between operations  13.5 us (1%)
    all_gather x1, blocking collectives, body(): prompt_rows = lax.all_gather(prompt, 'section', axis=0, tiled=True)  89 us
    psum x7, blocking collectives, layer_step(): summed = lax.psum(contract_last(hidden, down_rows), 'tensor')  77.6 us
    all_to_all x1, waiting for transfers between devices, body(): lax.all_to_all(lax.all_to_all(gate_right, 'tensor', split_axis=2, concat_...  74.6 us
    all_to_all x1, waiting for transfers between devices, body(): lax.all_to_all(lax.all_to_all(up_right, 'tensor', split_axis=2, concat_ax...  74.6 us
    dot_general x28, matrix products, contract_last(): lax.dot_general(left_side, right_side, (((1,), (1,)), ((), ())), preferre...  69.2 us
    all_to_all x1, blocking collectives, body(): lax.all_to_all(gate_left, 'section', split_axis=0, concat_axis=2, tiled=T...  54 us
    all_to_all x1, blocking collectives, body(): lax.all_to_all(up_left, 'section', split_axis=0, concat_axis=2, tiled=True)  51 us
    all_to_all x1, blocking collectives, body(): lax.all_to_all(down_left, 'tensor', split_axis=2, concat_axis=1, tiled=True)  48.1 us
  transfers between devices with their start and end apart: 14, of which 13 were waited for; matrix products, arithmetic and copies ran while one was open for 8% of the time, Pallas kernels for 0%

commit v1 on v0

v1 whole, which is shorter than its diff:
```python
import jax
import jax.numpy as jnp
from jax import lax
from jax.sharding import PartitionSpec as P

CORES = 2


def dot(left_side, right_side):
    return jnp.dot(left_side, right_side, preferred_element_type=jnp.float32)


def dot_last(left_side, right_side):
    return lax.dot_general(
        left_side, right_side, (((1,), (1,)), ((), ())), preferred_element_type=jnp.float32
    )


def swap_cores(block):
    ranks = range(lax.axis_size("tensor"))
    return lax.ppermute(block, "tensor", [(t, t ^ 1) for t in ranks])


def from_row(block, distance):
    tensor_count = lax.axis_size("tensor")
    shift = distance * CORES
    return lax.ppermute(
        block, "tensor", [(t, (t + shift) % tensor_count) for t in range(tensor_count)]
    )


def from_section(block, distance):
    count = lax.axis_size("section")
    return lax.ppermute(block, "section", [(s, (s + distance) % count) for s in range(count)])


def in_order(blocks, first, axis):
    count = len(blocks)
    if count == 1:
        return blocks[0]
    if count == 2:
        straight = jnp.concatenate(blocks, axis)
        turned = jnp.concatenate(blocks[::-1], axis)
        return jnp.where(first == 0, straight, turned)
    stacked = jnp.stack(blocks)
    places = (first - jnp.arange(count)) % count
    ordered = jnp.take(stacked, places, axis=0)
    return jnp.concatenate([ordered[i] for i in range(count)], axis)


def piece_of(block, index, count, axis):
    if count == 1:
        return block
    size = block.shape[axis] // count
    return lax.dynamic_slice_in_dim(block, index * size, size, axis)


def mirror(block, section_axis, tensor_axis):
    tensor_count, section_count = lax.axis_size("tensor"), lax.axis_size("section")
    ratio = tensor_count // section_count
    inner = lax.axis_index("tensor") % ratio
    arrived = []
    for shift in range(ratio):
        route = []
        for t in range(tensor_count):
            for s in range(section_count):
                target = ratio * s + (t % ratio + shift) % ratio
                route.append((t * section_count + s, target * section_count + t // ratio))
        piece = piece_of(block, (inner + shift) % ratio, ratio, section_axis)
        arrived.append(lax.ppermute(piece, ("tensor", "section"), route))
    return in_order(arrived, inner, tensor_axis)


def mirror_back(block, section_axis, tensor_axis):
    tensor_count, section_count = lax.axis_size("tensor"), lax.axis_size("section")
    ratio = tensor_count // section_count
    inner = lax.axis_index("tensor") % ratio
    arrived = []
    for shift in range(ratio):
        route = []
        for t in range(tensor_count):
            for s in range(section_count):
                target = ratio * s + (t % ratio + shift) % ratio
                route.append((t * section_count + s, target * section_count + t // ratio))
        piece = piece_of(block, (inner + shift) % ratio, ratio, tensor_axis)
        arrived.append(lax.ppermute(piece, ("tensor", "section"), route))
    return in_order(arrived, inner, section_axis)


def gather_rows(block, axis):
    rows = lax.axis_size("tensor") // CORES
    row = lax.axis_index("tensor") // CORES
    return in_order([block] + [from_row(block, k) for k in range(1, rows)], row, axis)


def gather_cores(block, axis):
    core = lax.axis_index("tensor") % CORES
    return in_order([block, swap_cores(block)], core, axis)


def sum_sections(block):
    total = block.astype(jnp.float32)
    arrived = [from_section(block, k) for k in range(1, lax.axis_size("section"))]
    for other in arrived:
        total = total + other.astype(jnp.float32)
    return total


def body(
    prompt, norm_gain, kept_ranks, gate_left, up_left, gate_right, up_right, down_left, down_right
):
    tensor_count, section_count = lax.axis_size("tensor"), lax.axis_size("section")
    tensor_rank, section_rank = lax.axis_index("tensor"), lax.axis_index("section")
    rows = tensor_count // CORES
    core, row = tensor_rank % CORES, tensor_rank // CORES
    layer_count = gate_left.shape[0]
    rank_block = gate_left.shape[1]
    width = norm_gain.shape[1]
    width_block = width // section_count
    ratio = tensor_count // section_count
    bf16, f32 = jnp.bfloat16, jnp.float32

    own = mirror(prompt, 0, 1)
    gain_piece = piece_of(norm_gain, tensor_rank, tensor_count, 1)
    settings = jnp.concatenate(
        [gain_piece, jnp.pad(kept_ranks.astype(f32), ((0, 0), (0, 125)))], 1
    )
    per_section = settings.shape[0]
    settings = mirror(jnp.tile(settings, (ratio, 1)), 0, 1)
    half = gather_rows(own, 0)
    settings = gather_rows(settings[None], 0)
    stream = gather_cores(half, 0)
    settings = gather_cores(settings[None], 0)
    first_right = mirror(down_right[:1], 2, 1)
    later_right = mirror(down_right[1:], 2, 1)

    column = jnp.arange(rank_block, dtype=jnp.int32) + tensor_rank * rank_block
    column = column.astype(f32)

    for layer in range(layer_count):
        owner = (layer // per_section) * ratio
        setting = settings[owner % CORES, owner // CORES, layer % per_section]
        parts = setting.reshape(ratio, -1)
        gain = parts[:, : width // tensor_count].reshape(-1)
        kept = parts[0, width // tensor_count :]

        float_stream = stream.astype(f32)
        squares = jnp.sum(float_stream * float_stream, -1, keepdims=True)
        high = squares.astype(bf16)
        low = (squares - high.astype(f32)).astype(bf16)
        weighted = (float_stream * gain).astype(bf16)
        gate_part = dot_last(weighted, gate_left[layer]).astype(bf16)
        up_part = dot_last(weighted, up_left[layer]).astype(bf16)
        tail = jnp.pad(jnp.concatenate([high, low], 1), ((0, 0), (0, 126)))
        total = sum_sections(jnp.concatenate([gate_part, up_part, tail], 1))
        squares = total[:, 2 * rank_block : 2 * rank_block + 1]
        squares = squares + total[:, 2 * rank_block + 1 : 2 * rank_block + 2]
        scale = lax.rsqrt(squares / width + 1e-05)
        gate_low = total[:, :rank_block] * scale * (column < kept[0]).astype(f32)
        up_low = total[:, rank_block : 2 * rank_block] * scale * (column < kept[1]).astype(f32)
        gate_low, up_low = gate_low.astype(bf16), up_low.astype(bf16)

        def products(side):
            gate = dot(gate_low, piece_of(gate_right[layer], side, CORES, 1))
            up = dot(up_low, piece_of(up_right[layer], side, CORES, 1))
            return jnp.stack([gate, up])

        sent = swap_cores(products(1 - core).astype(bf16))
        kept_sum = products(core) + sent.astype(f32)
        kept_low = kept_sum.astype(bf16)
        values = kept_low.astype(f32)
        for k in range(1, rows):
            values = values + from_row(kept_low, k).astype(f32)
        hidden = (jax.nn.silu(values[0]) * values[1]).astype(bf16)
        other = swap_cores(hidden)
        down = dot_last(hidden, piece_of(down_left[layer], core, CORES, 1))
        down = down + dot_last(other, piece_of(down_left[layer], 1 - core, CORES, 1))
        total = sum_sections(down.astype(bf16))
        down_low = (total * (column < kept[2]).astype(f32)).astype(bf16)

        right = first_right[0] if layer == 0 else later_right[layer - 1]
        kept_branch = dot_last(piece_of(down_low, core, CORES, 0), right)
        sent_branch = dot_last(piece_of(down_low, 1 - core, CORES, 0), right).astype(bf16)
        branch = (kept_branch + swap_cores(sent_branch).astype(f32)).astype(bf16)
        if layer < layer_count - 1:
            summed = half.astype(f32) + branch.astype(f32)
            for k in range(1, rows):
                summed = summed + from_row(branch, k).astype(f32)
            half = summed.astype(bf16)
            stream = gather_cores(half, 0)
        else:
            summed = piece_of(half, row, rows, 0).astype(f32)
            summed = summed + piece_of(branch, row, rows, 0).astype(f32)
            for k in range(1, rows):
                piece = piece_of(branch, (row + k) % rows, rows, 0)
                summed = summed + from_row(piece, k).astype(f32)
            return mirror_back(summed.astype(bf16), 0, 1)


def solution(mesh):
    in_specs = (
        P(("groups", "section"), "tensor"),
        P(("groups", "section"), None),
        P(("groups", "section"), None),
        P("groups", "tensor", "section"),
        P("groups", "tensor", "section"),
        P("groups", "tensor", "section"),
        P("groups", "tensor", "section"),
        P("groups", "tensor", "section"),
        P("groups", "tensor", "section"),
    )
    out_specs = P(("groups", "section"), "tensor")
    return jax.shard_map(body, mesh=mesh, in_specs=in_specs, out_specs=out_specs, check_vma=False)
```

time: 1010 us -> 287 us (0.28)
  blocking collectives: 433 us -> 0 us
  waiting for transfers between devices: 308 us -> 167 us
  local copies, waits for them, and re-layouts: 99.4 us -> 12.5 us
  matrix products: 73.3 us -> 23.9 us
  between operations: 13.5 us -> 1.05 us
    all_to_all x6 -> x0, waiting for transfers between devices: 257 us -> none  [the longest x1 74.6 us: body(): lax.all_to_all(lax.all_to_all(gate_right, 'tensor', split_axis=2, concat_...]
    all_gather x22 -> x0, blocking collectives: 202 us -> none  [the longest x1 89 us: body(): prompt_rows = lax.all_gather(prompt, 'section', axis=0, tiled=True)]
    ppermute x7 -> x56, waiting for transfers between devices: 13.2 us -> 167 us  [the longest x10 75.9 us: from_row(): lax.ppermute(block, 'tensor', [(t, (t + shift) % tensor_count) for t in r...]
    all_to_all x3 -> x0, blocking collectives: 153 us -> none  [the longest x1 54 us: body(): lax.all_to_all(gate_left, 'section', split_axis=0, concat_axis=2, tiled=T...]
    psum x7 -> x0, blocking collectives: 77.6 us -> none  [layer_step(): summed = lax.psum(contract_last(hidden, down_rows), 'tensor')]
    all_to_all x9 -> x0, local copies, waits for them, and re-layouts: 51.6 us -> none  [the longest x1 9.73 us: body(): lax.all_to_all(down_right, 'section', split_axis=0, concat_axis=2, tiled=...]
    dot_general x35 -> x40, matrix products: 73.3 us -> 23.9 us  [the longest x24 18.6 us: dot_last(): lax.dot_general(left_side, right_side, (((1,), (1,)), ((), ())), preferre...]
    unnamed x27 -> x43, local copies, waits for them, and re-layouts: 45.7 us -> 1.59 us
  transfers between devices with their start and end apart: 14 -> 56, of which waited for: 13 -> 48; matrix products, arithmetic and copies ran while one was open for 8% -> 9% of each run, Pallas kernels for 0% -> 0%
where the time goes in v1:
time: 287 us; the launch traced here: 286 us
  waiting for transfers between devices  167 us (58%)
  starting transfers between devices  67.3 us (23%)
  matrix products  23.9 us (8%)
  other arithmetic  14.6 us (5%)
  local copies, waits for them, and re-layouts  12.5 us (4%)
    ppermute x10, waiting for transfers between devices, from_row(): lax.ppermute(block, 'tensor', [(t, (t + shift) % tensor_count) for t in r...  75.9 us
    ppermute x4, waiting for transfers between devices, mirror(): arrived.append(lax.ppermute(piece, ('tensor', 'section'), route))  37.4 us
    ppermute x24, starting transfers between devices, from_section(): lax.ppermute(block, 'section', [(s, (s + distance) % count) for s in rang...  34.8 us
    ppermute x24, waiting for transfers between devices, from_section(): lax.ppermute(block, 'section', [(s, (s + distance) % count) for s in rang...  31.6 us
    dot_general x24, matrix products, dot_last(): lax.dot_general(left_side, right_side, (((1,), (1,)), ((), ())), preferre...  18.6 us
    ppermute x17, waiting for transfers between devices, swap_cores(): return lax.ppermute(block, 'tensor', [(t, t ^ 1) for t in ranks])  16.2 us
    ppermute x4, starting transfers between devices, mirror(): arrived.append(lax.ppermute(piece, ('tensor', 'section'), route))  15.9 us
    ppermute x10, starting transfers between devices, from_row(): lax.ppermute(block, 'tensor', [(t, (t + shift) % tensor_count) for t in r...  11.7 us
  transfers between devices with their start and end apart: 56, of which 48 were waited for; matrix products, arithmetic and copies ran while one was open for 9% of the time, Pallas kernels for 0%

profile of v1, /device:TPU:4, one launch (start us, length us, event | category | flops | bytes accessed | tf_op | source)
XLA Modules:
  0.0 285.9 jit_solution(3156315222960558866)
XLA Ops:
  0.0 4.6 %collective-permute-start = (bf16[16,2048]{1,0:T(8,128)(2,1)}, bf16[16,2048]{1,0:T(8,128)(2,1)S(1)}, u32[]{:S(2)}, u32[]{:S(2)}) collective-permute-start(bf16[16,2048]{1,0:T(8,128)(2,1)} %param.9), channel_id=1, source_target_pairs={{0,0},{1,4},{2,8},{3,12},{4,1},{5,5},{6,9},{7,13},{8,2},{9,6},{10,... | collective-permute-start | bytes 196616 | tf_op jit(solution)/shard_map/ppermute | solution.py:70
  5.3 3.5 %collective-permute-start.3 = (f32[1,2176]{1,0:T(1,128)S(1)}, f32[1,2176]{1,0:T(1,128)S(1)}, u32[]{:S(2)}, u32[]{:S(2)}) collective-permute-start(f32[1,2176]{1,0:T(1,128)S(1)} %fusion.191), channel_id=1, source_target_pairs={{0,0},{1,4},{2,8},{3,12},{4,1},{5,5},{6,9},{7,13},{8,2},{9,6},{10,... | collective-permute-start | bytes 26120 | tf_op jit(solution)/shard_map/ppermute | solution.py:70
  8.7 3.6 %fusion.216 = (bf16[1,128,3584]{2,1,0:T(8,128)(2,1)S(1)}, bf16[1,128,3584]{2,1,0:T(8,128)(2,1)}, bf16[1,128,3584]{2,1,0:T(8,128)(2,1)S(1)}, bf16[1,128,3584]{2,1,0:T(8,128)(2,1)}) fusion(bf16[4,128,3584]{2,1,0:T(8,128)(2,1)} %param.14), kind=kLoop, calls=%fused_computation.340 | loop fusion | bytes 7340032 | tf_op jit(solution)/shard_map/slice | solution.py:164
  12.9 1.6 fusion.217
  14.5 2.0 collective-permute-done.4
  18.7 3.5 %collective-permute-done.1 = bf16[16,2048]{1,0:T(8,128)(2,1)S(1)} collective-permute-done((bf16[16,2048]{1,0:T(8,128)(2,1)S(1)}, bf16[16,2048]{1,0:T(8,128)(2,1)S(1)}, u32[]{:S(2)}, u32[]{:S(2)}) %collective-permute-start.1) | collective-permute-done | bytes 65568 | tf_op jit(solution)/shard_map/ppermute | solution.py:27
  24.0 1.4 convolution_convert_fusion.18
  26.9 2.8 collective-permute-start.7
  31.2 2.1 collective-permute-done.6
  35.7 1.9 slice.263
  37.6 4.2 %collective-permute-start.15 = (bf16[1,2048,128]{2,1,0:T(8,128)(2,1)}, bf16[1,2048,128]{2,1,0:T(8,128)(2,1)}, u32[]{:S(2)}, u32[]{:S(2)}) collective-permute-start(bf16[1,2048,128]{2,1,0:T(8,128)(2,1)} %slice.263), channel_id=1, source_target_pairs={{0,0},{1,4},{2,8},{3,12},{4,1},{5,5},{6,9},{7,13},{8,2},{9,6},{10,... | collective-permute-start | bytes 1572872 | tf_op jit(solution)/shard_map/ppermute | solution.py:70
  42.1 1.4 convolution_bitcast_fusion.6
  44.6 3.3 %collective-permute-start.10 = (bf16[2,64,1792]{2,1,0:T(8,128)(2,1)S(1)}, bf16[2,64,1792]{2,1,0:T(8,128)(2,1)}, u32[]{:S(2)}, u32[]{:S(2)}) collective-permute-start(bf16[2,64,1792]{2,1,0:T(8,128)(2,1)S(1)} %fusion.16), channel_id=1, source_target_pairs={{0,8},{4,12},{8,0},{12,4},{1,9},{5,13},{9,1},{13,5},{2,10},{6,14},... | collective-permute-start | bytes 1376264 | tf_op jit(solution)/shard_map/ppermute | solution.py:27
  48.0 1.9 fusion.218
  49.9 18.5 %collective-permute-done.10 = bf16[2,64,1792]{2,1,0:T(8,128)(2,1)} collective-permute-done((bf16[2,64,1792]{2,1,0:T(8,128)(2,1)S(1)}, bf16[2,64,1792]{2,1,0:T(8,128)(2,1)}, u32[]{:S(2)}, u32[]{:S(2)}) %collective-permute-start.10) | collective-permute-done | bytes 458784 | tf_op jit(solution)/shard_map/ppermute | solution.py:27
  72.9 2.7 collective-permute-start.14
  83.1 4.5 %collective-permute-done.17 = bf16[32,2048]{1,0:T(8,128)(2,1)S(1)} collective-permute-done((bf16[32,2048]{1,0:T(8,128)(2,1)S(1)}, bf16[32,2048]{1,0:T(8,128)(2,1)S(1)}, u32[]{:S(2)}, u32[]{:S(2)}) %collective-permute-start.17) | collective-permute-done | bytes 131104 | tf_op jit(solution)/shard_map/ppermute | solution.py:27
  89.4 1.4 convolution_convert_fusion.17
  92.2 2.1 collective-permute-start.19
  94.3 1.8 collective-permute-start.20
  97.3 1.4 collective-permute-done.19
  98.7 1.5 collective-permute-done.20
  104.1 3.7 %collective-permute-start.28 = (bf16[3,2048,128]{2,1,0:T(8,128)(2,1)S(1)}, bf16[3,2048,128]{2,1,0:T(8,128)(2,1)S(1)}, u32[]{:S(2)}, u32[]{:S(2)}) collective-permute-start(bf16[3,2048,128]{2,1,0:T(8,128)(2,1)S(1)} %slice.280), channel_id=1, source_target_pairs={{0,0},{1,4},{2,8},{3,12},{4,1},{5,5},{6,9},{7,13},{8,2},{9,6},{10,... | collective-permute-start | bytes 4718600 | tf_op jit(solution)/shard_map/ppermute | solution.py:70
  107.8 12.3 %collective-permute-done.23 = bf16[2,64,1792]{2,1,0:T(8,128)(2,1)S(1)} collective-permute-done((bf16[2,64,1792]{2,1,0:T(8,128)(2,1)S(1)}, bf16[2,64,1792]{2,1,0:T(8,128)(2,1)S(1)}, u32[]{:S(2)}, u32[]{:S(2)}) %collective-permute-start.23) | collective-permute-done | bytes 458784 | tf_op jit(solution)/shard_map/ppermute | solution.py:27
  122.2 3.7 %collective-permute-start.25 = (bf16[64,128]{1,0:T(8,128)(2,1)S(1)}, bf16[64,128]{1,0:T(8,128)(2,1)S(1)}, u32[]{:S(2)}, u32[]{:S(2)}) collective-permute-start(bf16[64,128]{1,0:T(8,128)(2,1)S(1)} %fusion.13), channel_id=1, source_target_pairs={{0,1},{1,2},{2,3},{3,0},{4,5},{5,6},{6,7},{7,4},{8,9},{9,10},{10,1... | collective-permute-start | bytes 49160 | tf_op jit(solution)/shard_map/ppermute | solution.py:34
  125.8 2.4 collective-permute-start.27
  128.9 13.0 %collective-permute-done.25 = bf16[64,128]{1,0:T(8,128)(2,1)S(1)} collective-permute-done((bf16[64,128]{1,0:T(8,128)(2,1)S(1)}, bf16[64,128]{1,0:T(8,128)(2,1)S(1)}, u32[]{:S(2)}, u32[]{:S(2)}) %collective-permute-start.25) | collective-permute-done | bytes 16416 | tf_op jit(solution)/shard_map/ppermute | solution.py:34
  142.6 36.8 %collective-permute-done.28 = bf16[3,2048,128]{2,1,0:T(8,128)(2,1)S(1)} collective-permute-done((bf16[3,2048,128]{2,1,0:T(8,128)(2,1)S(1)}, bf16[3,2048,128]{2,1,0:T(8,128)(2,1)S(1)}, u32[]{:S(2)}, u32[]{:S(2)}) %collective-permute-start.28) | collective-permute-done | bytes 1572896 | tf_op jit(solution)/shard_map/ppermute | solution.py:70
  182.3 4.8 %collective-permute-done.30 = bf16[32,2048]{1,0:T(8,128)(2,1)S(1)} collective-permute-done((bf16[32,2048]{1,0:T(8,128)(2,1)S(1)}, bf16[32,2048]{1,0:T(8,128)(2,1)S(1)}, u32[]{:S(2)}, u32[]{:S(2)}) %collective-permute-start.30) | collective-permute-done | bytes 131104 | tf_op jit(solution)/shard_map/ppermute | solution.py:27
  189.3 1.7 convolution_convert_fusion.15
  191.1 1.6 convolution_convert_fusion.14
  192.8 1.4 collective-permute-start.33
  194.1 2.5 collective-permute-start.34
  197.2 2.1 collective-permute-done.32
  202.8 1.7 collective-permute-start.36
  204.5 10.9 %collective-permute-done.36 = bf16[2,64,1792]{2,1,0:T(8,128)(2,1)S(1)} collective-permute-done((bf16[2,64,1792]{2,1,0:T(8,128)(2,1)S(1)}, bf16[2,64,1792]{2,1,0:T(8,128)(2,1)S(1)}, u32[]{:S(2)}, u32[]{:S(2)}) %collective-permute-start.36) | collective-permute-done | bytes 458784 | tf_op jit(solution)/shard_map/ppermute | solution.py:27
  217.5 1.6 collective-permute-start.38
  219.1 1.6 collective-permute-start.39
  227.3 4.7 %collective-permute-done.42 = bf16[32,2048]{1,0:T(8,128)(2,1)S(1)} collective-permute-done((bf16[32,2048]{1,0:T(8,128)(2,1)S(1)}, bf16[32,2048]{1,0:T(8,128)(2,1)S(1)}, u32[]{:S(2)}, u32[]{:S(2)}) %collective-permute-start.42) | collective-permute-done | bytes 131104 | tf_op jit(solution)/shard_map/ppermute | solution.py:27
  234.3 1.6 convolution_convert_fusion.13
  236.0 1.6 convolution_convert_fusion.12
  238.8 2.3 collective-permute-start.45
  242.5 1.7 collective-permute-done.44
  249.6 11.5 %collective-permute-done.48 = bf16[2,64,1792]{2,1,0:T(8,128)(2,1)S(1)} collective-permute-done((bf16[2,64,1792]{2,1,0:T(8,128)(2,1)S(1)}, bf16[2,64,1792]{2,1,0:T(8,128)(2,1)S(1)}, u32[]{:S(2)}, u32[]{:S(2)}) %collective-permute-start.48) | collective-permute-done | bytes 458784 | tf_op jit(solution)/shard_map/ppermute | solution.py:27
  264.5 1.6 collective-permute-start.51
  273.1 3.1 %collective-permute-done.54 = bf16[16,2048]{1,0:T(8,128)(2,1)S(1)} collective-permute-done((bf16[16,2048]{1,0:T(8,128)(2,1)S(1)}, bf16[16,2048]{1,0:T(8,128)(2,1)S(1)}, u32[]{:S(2)}, u32[]{:S(2)}) %collective-permute-start.54) | collective-permute-done | bytes 65568 | tf_op jit(solution)/shard_map/ppermute | solution.py:27
  276.3 3.6 %collective-permute-start.55 = (bf16[16,2048]{1,0:T(8,128)(2,1)S(1)}, bf16[16,2048]{1,0:T(8,128)(2,1)S(1)}, u32[]{:S(2)}, u32[]{:S(2)}) collective-permute-start(bf16[16,2048]{1,0:T(8,128)(2,1)S(1)} %add_convert_fusion.3), channel_id=1, source_target_pairs={{0,0},{1,4},{2,8},{3,12},{4,1},{5,5},{6,9},{7,13},{8,2},{9,6},{10,... | collective-permute-start | bytes 196616 | tf_op jit(solution)/shard_map/ppermute | solution.py:86
  279.8 5.5 %collective-permute-done.55 = bf16[16,2048]{1,0:T(8,128)(2,1)S(1)} collective-permute-done((bf16[16,2048]{1,0:T(8,128)(2,1)S(1)}, bf16[16,2048]{1,0:T(8,128)(2,1)S(1)}, u32[]{:S(2)}, u32[]{:S(2)}) %collective-permute-start.55) | collective-permute-done | bytes 65568 | tf_op jit(solution)/shard_map/ppermute | solution.py:86
  (235 shorter events, 74.0 us)
Async XLA Ops:
  0.0 17.8 %collective-permute-start = (bf16[16,2048]{1,0:T(8,128)(2,1)}, bf16[16,2048]{1,0:T(8,128)(2,1)S(1)}, u32[]{:S(2)}, u32[]{:S(2)}) collective-permute-start(bf16[16,2048]{1,0:T(8,128)(2,1)} %param.9), channel_id=1, source_target_pairs={{0,0},{1,4},{2,8},{3,12},{4,1},{5,5},{6,9},{7,13},{8,2},{9,6},{10,... | collective-permute-start | bytes 196616 | tf_op jit(solution)/shard_map/ppermute | solution.py:70
  5.3 7.6 %collective-permute-start.3 = (f32[1,2176]{1,0:T(1,128)S(1)}, f32[1,2176]{1,0:T(1,128)S(1)}, u32[]{:S(2)}, u32[]{:S(2)}) collective-permute-start(f32[1,2176]{1,0:T(1,128)S(1)} %fusion.191), channel_id=1, source_target_pairs={{0,0},{1,4},{2,8},{3,12},{4,1},{5,5},{6,9},{7,13},{8,2},{9,6},{10,... | collective-permute-start | bytes 26120 | tf_op jit(solution)/shard_map/ppermute | solution.py:70
  12.9 3.7 %collective-permute-start.4 = (f32[1,1,2176]{2,0,1:T(1,128)S(1)}, f32[1,1,2176]{2,0,1:T(1,128)S(1)}, u32[]{:S(2)}, u32[]{:S(2)}) collective-permute-start(f32[1,1,2176]{2,0,1:T(1,128)S(1)} %bitcast.286), channel_id=1, source_target_pairs={{0,8},{4,12},{8,0},{12,4},{1,9},{5,13},{9,1},{13,5},{2,10},{6,14},... | collective-permute-start | bytes 26120 | tf_op jit(solution)/shard_map/ppermute | solution.py:27
  17.9 4.4 %collective-permute-start.1 = (bf16[16,2048]{1,0:T(8,128)(2,1)S(1)}, bf16[16,2048]{1,0:T(8,128)(2,1)S(1)}, u32[]{:S(2)}, u32[]{:S(2)}) collective-permute-start(bf16[16,2048]{1,0:T(8,128)(2,1)S(1)} %collective-permute-done), channel_id=1, source_target_pairs={{0,8},{4,12},{8,0},{12,4},{1,9},{5,13},{9,1},{13,5},{2,10},{6,14},... | collective-permute-start | bytes 196616 | tf_op jit(solution)/shard_map/ppermute | solution.py:27
  26.8 6.6 %collective-permute-start.6 = (bf16[64,384]{1,0:T(8,128)(2,1)S(1)}, bf16[64,384]{1,0:T(8,128)(2,1)S(1)}, u32[]{:S(2)}, u32[]{:S(2)}) collective-permute-start(bf16[64,384]{1,0:T(8,128)(2,1)S(1)} %fusion.130), channel_id=1, source_target_pairs={{0,1},{1,2},{2,3},{3,0},{4,5},{5,6},{6,7},{7,4},{8,9},{9,10},{10,1... | collective-permute-start | bytes 147464 | tf_op jit(solution)/shard_map/ppermute | solution.py:34
  26.9 7.2 %collective-permute-start.7 = (bf16[64,384]{1,0:T(8,128)(2,1)S(1)}, bf16[64,384]{1,0:T(8,128)(2,1)S(1)}, u32[]{:S(2)}, u32[]{:S(2)}) collective-permute-start(bf16[64,384]{1,0:T(8,128)(2,1)S(1)} %fusion.130), channel_id=1, source_target_pairs={{0,2},{1,3},{2,0},{3,1},{4,6},{5,7},{6,4},{7,5},{8,10},{9,11},{10,... | collective-permute-start | bytes 147464 | tf_op jit(solution)/shard_map/ppermute | solution.py:34
  29.7 4.4 %collective-permute-start.8 = (bf16[64,384]{1,0:T(8,128)(2,1)S(1)}, bf16[64,384]{1,0:T(8,128)(2,1)S(1)}, u32[]{:S(2)}, u32[]{:S(2)}) collective-permute-start(bf16[64,384]{1,0:T(8,128)(2,1)S(1)} %fusion.130), channel_id=1, source_target_pairs={{0,3},{1,0},{2,1},{3,2},{4,7},{5,4},{6,5},{7,6},{8,11},{9,8},{10,9... | collective-permute-start | bytes 147464 | tf_op jit(solution)/shard_map/ppermute | solution.py:34
  35.7 7.8 %collective-permute-start.9 = (bf16[2,64,1792]{2,1,0:T(8,128)(2,1)}, bf16[2,64,1792]{2,1,0:T(8,128)(2,1)}, u32[]{:S(2)}, u32[]{:S(2)}) collective-permute-start(bf16[2,64,1792]{2,1,0:T(8,128)(2,1)} %pad_maximum_fusion), channel_id=1, source_target_pairs={{0,4},{4,0},{8,12},{12,8},{1,5},{5,1},{9,13},{13,9},{2,6},{6,2},{1... | collective-permute-start | bytes 1376264 | tf_op jit(solution)/shard_map/ppermute | solution.py:21
  37.6 40.3 %collective-permute-start.15 = (bf16[1,2048,128]{2,1,0:T(8,128)(2,1)}, bf16[1,2048,128]{2,1,0:T(8,128)(2,1)}, u32[]{:S(2)}, u32[]{:S(2)}) collective-permute-start(bf16[1,2048,128]{2,1,0:T(8,128)(2,1)} %slice.263), channel_id=1, source_target_pairs={{0,0},{1,4},{2,8},{3,12},{4,1},{5,5},{6,9},{7,13},{8,2},{9,6},{10,... | collective-permute-start | bytes 1572872 | tf_op jit(solution)/shard_map/ppermute | solution.py:70
  44.6 23.8 %collective-permute-start.10 = (bf16[2,64,1792]{2,1,0:T(8,128)(2,1)S(1)}, bf16[2,64,1792]{2,1,0:T(8,128)(2,1)}, u32[]{:S(2)}, u32[]{:S(2)}) collective-permute-start(bf16[2,64,1792]{2,1,0:T(8,128)(2,1)S(1)} %fusion.16), channel_id=1, source_target_pairs={{0,8},{4,12},{8,0},{12,4},{1,9},{5,13},{9,1},{13,5},{2,10},{6,14},... | collective-permute-start | bytes 1376264 | tf_op jit(solution)/shard_map/ppermute | solution.py:27
  69.9 1.6 collective-permute-start.11
  71.7 5.6 %collective-permute-start.12 = (bf16[64,128]{1,0:T(8,128)(2,1)S(1)}, bf16[64,128]{1,0:T(8,128)(2,1)S(1)}, u32[]{:S(2)}, u32[]{:S(2)}) collective-permute-start(bf16[64,128]{1,0:T(8,128)(2,1)S(1)} %fusion.12), channel_id=1, source_target_pairs={{0,1},{1,2},{2,3},{3,0},{4,5},{5,6},{6,7},{7,4},{8,9},{9,10},{10,1... | collective-permute-start | bytes 49160 | tf_op jit(solution)/shard_map/ppermute | solution.py:34
  71.8 5.5 %collective-permute-start.13 = (bf16[64,128]{1,0:T(8,128)(2,1)S(1)}, bf16[64,128]{1,0:T(8,128)(2,1)S(1)}, u32[]{:S(2)}, u32[]{:S(2)}) collective-permute-start(bf16[64,128]{1,0:T(8,128)(2,1)S(1)} %fusion.12), channel_id=1, source_target_pairs={{0,2},{1,3},{2,0},{3,1},{4,6},{5,7},{6,4},{7,5},{8,10},{9,11},{10,... | collective-permute-start | bytes 49160 | tf_op jit(solution)/shard_map/ppermute | solution.py:34
  72.9 5.0 %collective-permute-start.14 = (bf16[64,128]{1,0:T(8,128)(2,1)S(1)}, bf16[64,128]{1,0:T(8,128)(2,1)S(1)}, u32[]{:S(2)}, u32[]{:S(2)}) collective-permute-start(bf16[64,128]{1,0:T(8,128)(2,1)S(1)} %fusion.12), channel_id=1, source_target_pairs={{0,3},{1,0},{2,1},{3,2},{4,7},{5,4},{6,5},{7,6},{8,11},{9,8},{10,9... | collective-permute-start | bytes 49160 | tf_op jit(solution)/shard_map/ppermute | solution.py:34
  79.2 1.4 collective-permute-start.16
  82.0 5.6 %collective-permute-start.17 = (bf16[32,2048]{1,0:T(8,128)(2,1)S(1)}, bf16[32,2048]{1,0:T(8,128)(2,1)S(1)}, u32[]{:S(2)}, u32[]{:S(2)}) collective-permute-start(bf16[32,2048]{1,0:T(8,128)(2,1)S(1)} %fusion.8), channel_id=1, source_target_pairs={{0,8},{4,12},{8,0},{12,4},{1,9},{5,13},{9,1},{13,5},{2,10},{6,14},... | collective-permute-start | bytes 393224 | tf_op jit(solution)/shard_map/ppermute | solution.py:27
  92.2 6.4 %collective-permute-start.19 = (bf16[64,384]{1,0:T(8,128)(2,1)S(1)}, bf16[64,384]{1,0:T(8,128)(2,1)S(1)}, u32[]{:S(2)}, u32[]{:S(2)}) collective-permute-start(bf16[64,384]{1,0:T(8,128)(2,1)S(1)} %fusion.131), channel_id=1, source_target_pairs={{0,1},{1,2},{2,3},{3,0},{4,5},{5,6},{6,7},{7,4},{8,9},{9,10},{10,1... | collective-permute-start | bytes 147464 | tf_op jit(solution)/shard_map/ppermute | solution.py:34
  94.3 5.9 %collective-permute-start.20 = (bf16[64,384]{1,0:T(8,128)(2,1)S(1)}, bf16[64,384]{1,0:T(8,128)(2,1)S(1)}, u32[]{:S(2)}, u32[]{:S(2)}) collective-permute-start(bf16[64,384]{1,0:T(8,128)(2,1)S(1)} %fusion.131), channel_id=1, source_target_pairs={{0,2},{1,3},{2,0},{3,1},{4,6},{5,7},{6,4},{7,5},{8,10},{9,11},{10,... | collective-permute-start | bytes 147464 | tf_op jit(solution)/shard_map/ppermute | solution.py:34
  96.1 4.5 %collective-permute-start.21 = (bf16[64,384]{1,0:T(8,128)(2,1)S(1)}, bf16[64,384]{1,0:T(8,128)(2,1)S(1)}, u32[]{:S(2)}, u32[]{:S(2)}) collective-permute-start(bf16[64,384]{1,0:T(8,128)(2,1)S(1)} %fusion.131), channel_id=1, source_target_pairs={{0,3},{1,0},{2,1},{3,2},{4,7},{5,4},{6,5},{7,6},{8,11},{9,8},{10,9... | collective-permute-start | bytes 147464 | tf_op jit(solution)/shard_map/ppermute | solution.py:34
  101.5 1.9 collective-permute-start.22
  103.4 16.6 %collective-permute-start.23 = (bf16[2,64,1792]{2,1,0:T(8,128)(2,1)S(1)}, bf16[2,64,1792]{2,1,0:T(8,128)(2,1)S(1)}, u32[]{:S(2)}, u32[]{:S(2)}) collective-permute-start(bf16[2,64,1792]{2,1,0:T(8,128)(2,1)S(1)} %fusion.17), channel_id=1, source_target_pairs={{0,8},{4,12},{8,0},{12,4},{1,9},{5,13},{9,1},{13,5},{2,10},{6,14},... | collective-permute-start | bytes 1376264 | tf_op jit(solution)/shard_map/ppermute | solution.py:27
  104.1 75.4 %collective-permute-start.28 = (bf16[3,2048,128]{2,1,0:T(8,128)(2,1)S(1)}, bf16[3,2048,128]{2,1,0:T(8,128)(2,1)S(1)}, u32[]{:S(2)}, u32[]{:S(2)}) collective-permute-start(bf16[3,2048,128]{2,1,0:T(8,128)(2,1)S(1)} %slice.280), channel_id=1, source_target_pairs={{0,0},{1,4},{2,8},{3,12},{4,1},{5,5},{6,9},{7,13},{8,2},{9,6},{10,... | collective-permute-start | bytes 4718600 | tf_op jit(solution)/shard_map/ppermute | solution.py:70
  120.3 1.6 collective-permute-start.24
  122.2 19.7 %collective-permute-start.25 = (bf16[64,128]{1,0:T(8,128)(2,1)S(1)}, bf16[64,128]{1,0:T(8,128)(2,1)S(1)}, u32[]{:S(2)}, u32[]{:S(2)}) collective-permute-start(bf16[64,128]{1,0:T(8,128)(2,1)S(1)} %fusion.13), channel_id=1, source_target_pairs={{0,1},{1,2},{2,3},{3,0},{4,5},{5,6},{6,7},{7,4},{8,9},{9,10},{10,1... | collective-permute-start | bytes 49160 | tf_op jit(solution)/shard_map/ppermute | solution.py:34
  125.8 16.4 %collective-permute-start.26 = (bf16[64,128]{1,0:T(8,128)(2,1)S(1)}, bf16[64,128]{1,0:T(8,128)(2,1)S(1)}, u32[]{:S(2)}, u32[]{:S(2)}) collective-permute-start(bf16[64,128]{1,0:T(8,128)(2,1)S(1)} %fusion.13), channel_id=1, source_target_pairs={{0,2},{1,3},{2,0},{3,1},{4,6},{5,7},{6,4},{7,5},{8,10},{9,11},{10,... | collective-permute-start | bytes 49160 | tf_op jit(solution)/shard_map/ppermute | solution.py:34
  125.8 16.8 %collective-permute-start.27 = (bf16[64,128]{1,0:T(8,128)(2,1)S(1)}, bf16[64,128]{1,0:T(8,128)(2,1)S(1)}, u32[]{:S(2)}, u32[]{:S(2)}) collective-permute-start(bf16[64,128]{1,0:T(8,128)(2,1)S(1)} %fusion.13), channel_id=1, source_target_pairs={{0,3},{1,0},{2,1},{3,2},{4,7},{5,4},{6,5},{7,6},{8,11},{9,8},{10,9... | collective-permute-start | bytes 49160 | tf_op jit(solution)/shard_map/ppermute | solution.py:34
  181.4 5.6 %collective-permute-start.30 = (bf16[32,2048]{1,0:T(8,128)(2,1)S(1)}, bf16[32,2048]{1,0:T(8,128)(2,1)S(1)}, u32[]{:S(2)}, u32[]{:S(2)}) collective-permute-start(bf16[32,2048]{1,0:T(8,128)(2,1)S(1)} %fusion.9), channel_id=1, source_target_pairs={{0,8},{4,12},{8,0},{12,4},{1,9},{5,13},{9,1},{13,5},{2,10},{6,14},... | collective-permute-start | bytes 393224 | tf_op jit(solution)/shard_map/ppermute | solution.py:27
  192.7 6.6 %collective-permute-start.32 = (bf16[64,384]{1,0:T(8,128)(2,1)S(1)}, bf16[64,384]{1,0:T(8,128)(2,1)S(1)}, u32[]{:S(2)}, u32[]{:S(2)}) collective-permute-start(bf16[64,384]{1,0:T(8,128)(2,1)S(1)} %fusion.132), channel_id=1, source_target_pairs={{0,1},{1,2},{2,3},{3,0},{4,5},{5,6},{6,7},{7,4},{8,9},{9,10},{10,1... | collective-permute-start | bytes 147464 | tf_op jit(solution)/shard_map/ppermute | solution.py:34
  192.8 7.2 %collective-permute-start.33 = (bf16[64,384]{1,0:T(8,128)(2,1)S(1)}, bf16[64,384]{1,0:T(8,128)(2,1)S(1)}, u32[]{:S(2)}, u32[]{:S(2)}) collective-permute-start(bf16[64,384]{1,0:T(8,128)(2,1)S(1)} %fusion.132), channel_id=1, source_target_pairs={{0,2},{1,3},{2,0},{3,1},{4,6},{5,7},{6,4},{7,5},{8,10},{9,11},{10,... | collective-permute-start | bytes 147464 | tf_op jit(solution)/shard_map/ppermute | solution.py:34
  194.1 5.8 %collective-permute-start.34 = (bf16[64,384]{1,0:T(8,128)(2,1)S(1)}, bf16[64,384]{1,0:T(8,128)(2,1)S(1)}, u32[]{:S(2)}, u32[]{:S(2)}) collective-permute-start(bf16[64,384]{1,0:T(8,128)(2,1)S(1)} %fusion.132), channel_id=1, source_target_pairs={{0,3},{1,0},{2,1},{3,2},{4,7},{5,4},{6,5},{7,6},{8,11},{9,8},{10,9... | collective-permute-start | bytes 147464 | tf_op jit(solution)/shard_map/ppermute | solution.py:34
  200.8 1.9 collective-permute-start.35
  202.8 12.6 %collective-permute-start.36 = (bf16[2,64,1792]{2,1,0:T(8,128)(2,1)S(1)}, bf16[2,64,1792]{2,1,0:T(8,128)(2,1)S(1)}, u32[]{:S(2)}, u32[]{:S(2)}) collective-permute-start(bf16[2,64,1792]{2,1,0:T(8,128)(2,1)S(1)} %fusion.18), channel_id=1, source_target_pairs={{0,8},{4,12},{8,0},{12,4},{1,9},{5,13},{9,1},{13,5},{2,10},{6,14},... | collective-permute-start | bytes 1376264 | tf_op jit(solution)/shard_map/ppermute | solution.py:27
  215.7 1.6 collective-permute-start.37
  217.5 5.6 %collective-permute-start.38 = (bf16[64,128]{1,0:T(8,128)(2,1)S(1)}, bf16[64,128]{1,0:T(8,128)(2,1)S(1)}, u32[]{:S(2)}, u32[]{:S(2)}) collective-permute-start(bf16[64,128]{1,0:T(8,128)(2,1)S(1)} %fusion.14), channel_id=1, source_target_pairs={{0,1},{1,2},{2,3},{3,0},{4,5},{5,6},{6,7},{7,4},{8,9},{9,10},{10,1... | collective-permute-start | bytes 49160 | tf_op jit(solution)/shard_map/ppermute | solution.py:34
  219.1 4.8 %collective-permute-start.39 = (bf16[64,128]{1,0:T(8,128)(2,1)S(1)}, bf16[64,128]{1,0:T(8,128)(2,1)S(1)}, u32[]{:S(2)}, u32[]{:S(2)}) collective-permute-start(bf16[64,128]{1,0:T(8,128)(2,1)S(1)} %fusion.14), channel_id=1, source_target_pairs={{0,2},{1,3},{2,0},{3,1},{4,6},{5,7},{6,4},{7,5},{8,10},{9,11},{10,... | collective-permute-start | bytes 49160 | tf_op jit(solution)/shard_map/ppermute | solution.py:34
  220.7 3.7 %collective-permute-start.40 = (bf16[64,128]{1,0:T(8,128)(2,1)S(1)}, bf16[64,128]{1,0:T(8,128)(2,1)S(1)}, u32[]{:S(2)}, u32[]{:S(2)}) collective-permute-start(bf16[64,128]{1,0:T(8,128)(2,1)S(1)} %fusion.14), channel_id=1, source_target_pairs={{0,3},{1,0},{2,1},{3,2},{4,7},{5,4},{6,5},{7,6},{8,11},{9,8},{10,9... | collective-permute-start | bytes 49160 | tf_op jit(solution)/shard_map/ppermute | solution.py:34
  226.5 5.6 %collective-permute-start.42 = (bf16[32,2048]{1,0:T(8,128)(2,1)S(1)}, bf16[32,2048]{1,0:T(8,128)(2,1)S(1)}, u32[]{:S(2)}, u32[]{:S(2)}) collective-permute-start(bf16[32,2048]{1,0:T(8,128)(2,1)S(1)} %fusion.10), channel_id=1, source_target_pairs={{0,8},{4,12},{8,0},{12,4},{1,9},{5,13},{9,1},{13,5},{2,10},{6,14},... | collective-permute-start | bytes 393224 | tf_op jit(solution)/shard_map/ppermute | solution.py:27
  237.6 6.6 %collective-permute-start.44 = (bf16[64,384]{1,0:T(8,128)(2,1)S(1)}, bf16[64,384]{1,0:T(8,128)(2,1)S(1)}, u32[]{:S(2)}, u32[]{:S(2)}) collective-permute-start(bf16[64,384]{1,0:T(8,128)(2,1)S(1)} %fusion.133), channel_id=1, source_target_pairs={{0,1},{1,2},{2,3},{3,0},{4,5},{5,6},{6,7},{7,4},{8,9},{9,10},{10,1... | collective-permute-start | bytes 147464 | tf_op jit(solution)/shard_map/ppermute | solution.py:34
  238.8 6.6 %collective-permute-start.45 = (bf16[64,384]{1,0:T(8,128)(2,1)S(1)}, bf16[64,384]{1,0:T(8,128)(2,1)S(1)}, u32[]{:S(2)}, u32[]{:S(2)}) collective-permute-start(bf16[64,384]{1,0:T(8,128)(2,1)S(1)} %fusion.133), channel_id=1, source_target_pairs={{0,2},{1,3},{2,0},{3,1},{4,6},{5,7},{6,4},{7,5},{8,10},{9,11},{10,... | collective-permute-start | bytes 147464 | tf_op jit(solution)/shard_map/ppermute | solution.py:34
  241.1 4.6 %collective-permute-start.46 = (bf16[64,384]{1,0:T(8,128)(2,1)S(1)}, bf16[64,384]{1,0:T(8,128)(2,1)S(1)}, u32[]{:S(2)}, u32[]{:S(2)}) collective-permute-start(bf16[64,384]{1,0:T(8,128)(2,1)S(1)} %fusion.133), channel_id=1, source_target_pairs={{0,3},{1,0},{2,1},{3,2},{4,7},{5,4},{6,5},{7,6},{8,11},{9,8},{10,9... | collective-permute-start | bytes 147464 | tf_op jit(solution)/shard_map/ppermute | solution.py:34
  246.6 1.9 collective-permute-start.47
  248.5 12.6 %collective-permute-start.48 = (bf16[2,64,1792]{2,1,0:T(8,128)(2,1)S(1)}, bf16[2,64,1792]{2,1,0:T(8,128)(2,1)S(1)}, u32[]{:S(2)}, u32[]{:S(2)}) collective-permute-start(bf16[2,64,1792]{2,1,0:T(8,128)(2,1)S(1)} %fusion.19), channel_id=1, source_target_pairs={{0,8},{4,12},{8,0},{12,4},{1,9},{5,13},{9,1},{13,5},{2,10},{6,14},... | collective-permute-start | bytes 1376264 | tf_op jit(solution)/shard_map/ppermute | solution.py:27
  261.4 1.6 collective-permute-start.49
  263.3 5.6 %collective-permute-start.50 = (bf16[64,128]{1,0:T(8,128)(2,1)S(1)}, bf16[64,128]{1,0:T(8,128)(2,1)S(1)}, u32[]{:S(2)}, u32[]{:S(2)}) collective-permute-start(bf16[64,128]{1,0:T(8,128)(2,1)S(1)} %fusion.15), channel_id=1, source_target_pairs={{0,1},{1,2},{2,3},{3,0},{4,5},{5,6},{6,7},{7,4},{8,9},{9,10},{10,1... | collective-permute-start | bytes 49160 | tf_op jit(solution)/shard_map/ppermute | solution.py:34
  264.5 4.7 %collective-permute-start.51 = (bf16[64,128]{1,0:T(8,128)(2,1)S(1)}, bf16[64,128]{1,0:T(8,128)(2,1)S(1)}, u32[]{:S(2)}, u32[]{:S(2)}) collective-permute-start(bf16[64,128]{1,0:T(8,128)(2,1)S(1)} %fusion.15), channel_id=1, source_target_pairs={{0,2},{1,3},{2,0},{3,1},{4,6},{5,7},{6,4},{7,5},{8,10},{9,11},{10,... | collective-permute-start | bytes 49160 | tf_op jit(solution)/shard_map/ppermute | solution.py:34
  266.2 3.7 %collective-permute-start.52 = (bf16[64,128]{1,0:T(8,128)(2,1)S(1)}, bf16[64,128]{1,0:T(8,128)(2,1)S(1)}, u32[]{:S(2)}, u32[]{:S(2)}) collective-permute-start(bf16[64,128]{1,0:T(8,128)(2,1)S(1)} %fusion.15), channel_id=1, source_target_pairs={{0,3},{1,0},{2,1},{3,2},{4,7},{5,4},{6,5},{7,6},{8,11},{9,8},{10,9... | collective-permute-start | bytes 49160 | tf_op jit(solution)/shard_map/ppermute | solution.py:34
  271.9 4.3 %collective-permute-start.54 = (bf16[16,2048]{1,0:T(8,128)(2,1)S(1)}, bf16[16,2048]{1,0:T(8,128)(2,1)S(1)}, u32[]{:S(2)}, u32[]{:S(2)}) collective-permute-start(bf16[16,2048]{1,0:T(8,128)(2,1)S(1)} %constant_dynamic-slice_fusion.2), channel_id=1, source_target_pairs={{0,8},{4,12},{8,0},{12,4},{1,9},{5,13},{9,1},{13,5},{2,10},{6,14},... | collective-permute-start | bytes 196616 | tf_op jit(solution)/shard_map/ppermute | solution.py:27
  276.3 9.1 %collective-permute-start.55 = (bf16[16,2048]{1,0:T(8,128)(2,1)S(1)}, bf16[16,2048]{1,0:T(8,128)(2,1)S(1)}, u32[]{:S(2)}, u32[]{:S(2)}) collective-permute-start(bf16[16,2048]{1,0:T(8,128)(2,1)S(1)} %add_convert_fusion.3), channel_id=1, source_target_pairs={{0,0},{1,4},{2,8},{3,12},{4,1},{5,5},{6,9},{7,13},{8,2},{9,6},{10,... | collective-permute-start | bytes 196616 | tf_op jit(solution)/shard_map/ppermute | solution.py:86
  (29 other events, 265.5 us)
